TPU v7x, 128 devices: a whole 4x4x4 slice. The times are simulated.
128 devices in a mesh: row: 8 (over y, core), col: 16 (over x, z).
Axes of the slice: x: 4, y: 4, z: 4, core: 2. Of those that a mesh axis runs over, the one named last changes fastest.
Arguments:
- theta: float32 [64, 256, 256], P('row', None, 'col'), may hold values from -6 to 6
- left_env: float32 [32, 32, 256, 256], P('row', 'col'), as said below
- right_env: float32 [8, 32, 256, 256], P(None, 'col'), as said below
- left_sector: int32 [64], replicated, may hold values from 0 to 31, as said below
- right_sector: int32 [64], P('row'), may hold values from 0 to 7
- term_on: int32 [64, 32], P('row', 'col'), may hold values 0 or 1
- left_size: int32 [32], replicated, may hold values from 1 to 256, 5120 in all
- right_size: int32 [8], replicated, may hold values from 1 to 256, 1280 in all
Outputs:
- new_theta: float32 [64, 256, 256], P('row', None, 'col')
- energy: float32 [], replicated
Inputs may be any that keep to these rules, and one draw needn't show every extreme that they name: `left_sector`: left sector s belongs to row s // 4. Block k belongs to row k // 8. The 8 blocks of one row name distinct left sectors; they name either none or exactly 2 sectors belonging to any one row, and the blocks of every row name 2 sectors belonging to one common row. `left_env`: each tile is symmetric in its last two dimensions. `right_env`: each tile is symmetric in its last two dimensions.
All inputs are finite; a program needn't handle non-finite values. No bound on the sum of `term_on` on one device may be relied on, other than what follows from the above.
Results may differ from a plain program's by a relative error of at most 0.0001.
Values sent between devices are 32-bit elements; how exact they have to be, the bound alone decides.
No kernel may reach another device: no remote copies, remote signals or barrier semaphores. Data moves between devices by JAX's collectives and lax.ppermute only.
A program may use at most 128 MiB of HBM per device.

v0:
```python
import jax
import jax.numpy as jnp
from jax import lax
from jax.sharding import PartitionSpec as P

ITERS = 2
highest = lax.Precision.HIGHEST


def lookup(small_table, index_list):
    slot_hits = index_list[:, None] == jnp.arange(small_table.shape[0], dtype=jnp.int32)[None, :]
    return jnp.sum(jnp.where(slot_hits, small_table[None, :], 0), axis=1)


def tile_masks(left_ids, right_ids, left_size, right_size, tile_size, offset, span_cols):
    rows_live = lookup(left_size, left_ids)
    cols_live = lookup(right_size, right_ids)
    row_mask = (jnp.arange(tile_size, dtype=jnp.int32)[None, :] < rows_live[:, None]).astype(
        jnp.float32
    )
    col_mask = (
        (offset + jnp.arange(span_cols, dtype=jnp.int32))[None, :] < cols_live[:, None]
    ).astype(jnp.float32)
    return row_mask[:, :, None] * col_mask[:, None, :]


def local(theta, left_env, right_env, left_sector, right_sector, term_on, left_size, right_size):
    row_count = lax.axis_size("row")
    blocks, tile_size, thin_cols = theta.shape
    local_sectors = left_env.shape[0]
    capacity = max(2, 2 * blocks // row_count)
    row_index = lax.axis_index("row")
    col_index = lax.axis_index("col")
    own_left = lax.dynamic_slice_in_dim(left_sector, row_index * blocks, blocks)
    offset = col_index * thin_cols
    span_cols = theta.shape[2]
    start_mask = tile_masks(
        own_left, right_sector, left_size, right_size, tile_size, offset, span_cols
    )
    start_vec = theta * start_mask
    senders = row_index * local_sectors + jnp.arange(local_sectors, dtype=jnp.int32)
    wanted = left_sector.reshape(row_count, blocks)
    used_flag = jnp.any(wanted[:, :, None] == senders[None, None, :], axis=1)
    used_count = used_flag.astype(jnp.int32)
    before = jnp.cumsum(used_count, axis=1) - used_count
    pick_flag = used_flag[:, None, :] & (
        before[:, None, :] == jnp.arange(capacity, dtype=jnp.int32)[None, :, None]
    )
    filled = jnp.any(pick_flag, axis=2).reshape(-1)
    local_index = jnp.sum(
        jnp.where(pick_flag, jnp.arange(local_sectors, dtype=jnp.int32)[None, None, :], 0), axis=2
    ).reshape(-1)
    outgoing = (
        jnp.take(left_env, local_index, axis=0) * filled.astype(jnp.float32)[:, None, None, None]
    )
    arrived = lax.all_to_all(outgoing, "row", split_axis=0, concat_axis=0, tiled=True)
    every_sector = jnp.arange(row_count * local_sectors, dtype=jnp.int32)
    needed = (
        jnp.any(own_left[:, None] == every_sector[None, :], axis=0)
        .astype(jnp.int32)
        .reshape(row_count, local_sectors)
    )
    order_rank = (jnp.cumsum(needed, axis=1) - needed).reshape(-1)
    position = own_left // local_sectors * capacity + lookup(order_rank, own_left)
    left_pick = jnp.take(arrived, position, axis=0)
    right_pick = jnp.take(right_env, right_sector, axis=0)
    weights = term_on.astype(jnp.float32)

    def contract(full_vector):
        middle = (
            jnp.einsum("swia,sab->swib", left_pick, full_vector, precision=highest)
            * weights[:, :, None, None]
        )
        return jnp.einsum("swib,swjb->sij", middle, right_pick, precision=highest)

    def operate(vector):
        full_vector = lax.all_gather(vector, "col", axis=2, tiled=True)
        total_sum = lax.psum_scatter(contract(full_vector), "col", scatter_dimension=2, tiled=True)
        return total_sum * start_mask

    def combine(values):
        reduced = lax.psum(values, ("row", "col"))
        return reduced

    image_vec = operate(start_vec)
    norm_sq, correlation = combine((jnp.sum(start_vec * start_vec), jnp.sum(start_vec * image_vec)))
    inv_norm = 1.0 / jnp.sqrt(norm_sq)
    basis_vec = start_vec * inv_norm
    applied = image_vec * inv_norm
    ritz_value = correlation / norm_sq
    for turn_index in range(ITERS):
        residual = applied - ritz_value * basis_vec
        (res_sq,) = combine((jnp.sum(residual * residual),))
        length = jnp.sqrt(res_sq)
        fresh_vec = residual / length
        fresh_applied = operate(fresh_vec)
        (curvature,) = combine((jnp.sum(fresh_vec * fresh_applied),))
        half_gap = 0.5 * (ritz_value - curvature)
        root_term = jnp.sqrt(half_gap * half_gap + res_sq)
        lowest = 0.5 * (ritz_value + curvature) - root_term
        first_coef = curvature - lowest
        pair_norm = jnp.sqrt(first_coef * first_coef + res_sq)
        basis_vec = (first_coef * basis_vec - length * fresh_vec) / pair_norm
        applied = (first_coef * applied - length * fresh_applied) / pair_norm
        ritz_value = lowest
    total_entries = blocks * row_count * tile_size * tile_size
    output = basis_vec * jnp.sqrt(jnp.float32(total_entries))
    return (output, ritz_value)


def solution(mesh):
    placed = (
        P("row", None, "col"),
        P("row", "col", None, None),
        P(None, "col", None, None),
        P(),
        P("row"),
        P("row", "col"),
        P(),
        P(),
    )
    return jax.shard_map(
        local, mesh=mesh, in_specs=placed, out_specs=(P("row", None, "col"), P()), check_vma=False
    )
```

profile of v0, /device:TPU:1, one launch (start us, length us, event | category | flops | bytes accessed | tf_op | source)
XLA Modules:
  0.0 820.7 jit_solution(7117098073512323360)
XLA Ops:
  7.2 0.0 copy-start
  7.2 0.9 eq.29
  8.1 0.2 compare_reduce_fusion
  8.4 0.1 copy.12
  8.5 0.1 reshape.147
  8.5 0.1 reshape.146
  8.7 0.1 copy.14
  8.8 0.1 reshape.149
  8.9 4.3 gather_fusion
  13.2 7.9 select_multiply_fusion
  21.1 0.0 copy-start.4
  21.1 0.0 copy-start.8
  21.1 6.4 all-to-all-start
  27.5 0.1 dynamic_slice.3
  27.6 0.1 fusion.51
  27.7 0.1 reshape.148
  27.8 0.2 reduce_window_sum.19
  27.9 0.1 reduce_window_sum.20
  28.0 0.2 select_reduce_fusion
  28.2 0.2 select_reduce_fusion.1
  28.4 0.1 compare_convert_fusion
  28.5 0.1 fusion.50
  28.6 0.7 multiply_multiply_fusion.3
  29.3 0.0 all-gather.4.cloned.1.call-update
  29.3 0.0 reduce-scatter.4.cloned.1.call-start
  29.4 0.1 copy.15
  29.5 4.9 gather_fusion.2
  34.4 0.1 compare_and_fusion.2
  34.5 86.8 %all-to-all-done = f32[16,2,256,256]{3,2,1,0:T(8,128)} async-done(((f32[16,2,256,256]{3,2,1,0:T(8,128)}), f32[16,2,256,256]{3,2,1,0:T(8,128)}, u32[]{:S(2)}, u32[]{:S(2)}) %all-to-all-start) | async-done | bytes 8388640 | tf_op jit(solution)/shard_map/all_to_all | solution.py:56
  121.4 6.2 gather_fusion.1
  127.6 6.8 fusion.13
  134.4 5.9 fusion.33
  140.2 0.0 reduce-scatter.4.cloned.1.call-update
  140.3 0.0 all-gather.6.cloned.1.call-start
  140.3 73.6 %reduce-scatter.4.cloned.1.call-done = f32[8,256,16]{1,2,0:T(8,128)} async-done(((f32[8,256,256]{1,2,0:T(8,128)}), f32[8,256,16]{1,2,0:T(8,128)}) %reduce-scatter.4.cloned.1.call-update) | async-done | bytes 131088 | tf_op jit(solution)/shard_map/reduce_scatter | solution.py:78
  213.9 1.6 multiply_reduce_fusion.4
  215.6 65.9 %all-reduce = (f32[]{:T(128)}, f32[]{:T(128)}) all-reduce(f32[]{:T(128)} %get-tuple-element.3, f32[]{:T(128)} %get-tuple-element.2), channel_id=1, replica_groups=mesh['row'=8,'col'=16] {'row','col'}, use_global_device_ids=true, to_apply=%region_13.14 | all-reduce | flops 2 | bytes 16 | tf_op jit(solution)/shard_map/psum | solution.py:82
  283.5 1.6 multiply_reduce_fusion.2
  285.1 62.7 %psum.44 = f32[]{:T(128)} all-reduce(f32[]{:T(128)} %multiply_reduce_fusion.2), channel_id=1, replica_groups=mesh['row'=8,'col'=16] {'row','col'}, use_global_device_ids=true, to_apply=%region_15.16 | all-reduce | flops 1 | bytes 8 | tf_op jit(solution)/shard_map/psum | solution.py:82
  348.5 1.7 broadcast_divide_fusion.1
  350.2 0.0 all-gather.6.cloned.1.call-update
  350.2 0.0 reduce-scatter.6.cloned.1.call-start
  350.2 41.4 %all-gather.6.cloned.1.call-done = f32[8,256,256]{1,2,0:T(8,128)} async-done(((f32[8,256,16]{1,2,0:T(8,128)}), f32[8,256,256]{1,2,0:T(8,128)}) %all-gather.6.cloned.1.call-update) | async-done | bytes 2097168 | tf_op jit(solution)/shard_map/all_gather | solution.py:77
  391.6 6.8 fusion.11
  398.4 0.0 copy-start.5
  398.5 5.9 fusion.38
  404.3 0.0 reduce-scatter.6.cloned.1.call-update
  404.4 0.0 all-gather.8.cloned.1.call-start
  404.4 73.2 %reduce-scatter.6.cloned.1.call-done = f32[8,256,16]{1,2,0:T(8,128)} async-done(((f32[8,256,256]{1,2,0:T(8,128)}), f32[8,256,16]{1,2,0:T(8,128)}) %reduce-scatter.6.cloned.1.call-update) | async-done | bytes 131088 | tf_op jit(solution)/shard_map/reduce_scatter | solution.py:78
  477.6 1.6 multiply_reduce_fusion.1
  479.2 65.8 %psum.45 = f32[]{:T(128)} all-reduce(f32[]{:T(128)} %multiply_reduce_fusion.1), channel_id=1, replica_groups=mesh['row'=8,'col'=16] {'row','col'}, use_global_device_ids=true, to_apply=%region_18.19 | all-reduce | flops 1 | bytes 8 | tf_op jit(solution)/shard_map/psum | solution.py:82
  548.3 1.7 multiply_reduce_fusion
  550.0 62.5 %psum.46 = f32[]{:T(128)} all-reduce(f32[]{:T(128)} %get-tuple-element.8), channel_id=1, replica_groups=mesh['row'=8,'col'=16] {'row','col'}, use_global_device_ids=true, to_apply=%region_20.21 | all-reduce | flops 1 | bytes 8 | tf_op jit(solution)/shard_map/psum | solution.py:82
  613.2 0.7 broadcast_divide_fusion
  613.9 0.0 all-gather.8.cloned.1.call-update
  613.9 0.3 reduce-scatter.8.cloned.1.call-start
  614.2 41.2 %all-gather.8.cloned.1.call-done = f32[8,256,256]{1,2,0:T(8,128)} async-done(((f32[8,256,16]{1,2,0:T(8,128)}), f32[8,256,256]{1,2,0:T(8,128)}) %all-gather.8.cloned.1.call-update) | async-done | bytes 2097168 | tf_op jit(solution)/shard_map/all_gather | solution.py:77
  655.3 6.8 fusion.9
  662.1 5.9 fusion.43
  668.0 0.0 reduce-scatter.8.cloned.1.call-update
  668.0 73.2 %reduce-scatter.8.cloned.1.call-done = f32[8,256,16]{1,2,0:T(8,128)} async-done(((f32[8,256,256]{1,2,0:T(8,128)}), f32[8,256,16]{1,2,0:T(8,128)}) %reduce-scatter.8.cloned.1.call-update) | async-done | bytes 131088 | tf_op jit(solution)/shard_map/reduce_scatter | solution.py:78
  741.3 1.6 fusion.49
  742.9 65.8 %psum.47 = f32[]{:T(128)} all-reduce(f32[]{:T(128)} %fusion.49), channel_id=1, replica_groups=mesh['row'=8,'col'=16] {'row','col'}, use_global_device_ids=true, to_apply=%region_23.24 | all-reduce | flops 1 | bytes 8 | tf_op jit(solution)/shard_map/psum | solution.py:82
  812.0 0.8 divide_multiply_fusion
  (40 shorter events, 0.2 us)
Async XLA Ops:
  7.2 1.7 copy-start
  21.1 6.4 copy-start.7
  21.1 6.9 copy-start.10
  21.1 7.0 copy-start.11
  21.1 7.1 copy-start.9
  21.1 7.5 copy-start.4
  21.1 8.3 %copy-start.8 = (s32[8,2]{0,1:T(2,128)S(1)}, s32[8,2]{0,1:T(2,128)}, u32[]{:S(2)}) copy-start(s32[8,2]{0,1:T(2,128)} %param.13) | copy-start | bytes 196
  21.1 100.3 %all-to-all-start = ((f32[16,2,256,256]{3,2,1,0:T(8,128)}), f32[16,2,256,256]{3,2,1,0:T(8,128)}, u32[]{:S(2)}, u32[]{:S(2)}) async-start(f32[16,2,256,256]{3,2,1,0:T(8,128)} %select_multiply_fusion), calls=%async_computation | async-start | bytes 16777216 | tf_op jit(solution)/shard_map/all_to_all | solution.py:56
  27.5 100.0 %all-gather.4.cloned.1.call-start = ((), (), s32[]{:S(2)}) async-start(), calls=%async_computation.4 | async-start | bytes 2228224 | tf_op jit(solution)/shard_map/all_gather | solution.py:77
  29.3 184.6 %reduce-scatter.4.cloned.1.call-start = ((), (), s32[]{:S(2)}) async-start(), calls=%async_computation.5 | async-start | bytes 2228224 | tf_op jit(solution)/shard_map/reduce_scatter | solution.py:78
  127.6 6.8 copy-start.1
  140.3 251.4 %all-gather.6.cloned.1.call-start = ((), (), s32[]{:S(2)}) async-start(), calls=%async_computation.6 | async-start | bytes 2228224 | tf_op jit(solution)/shard_map/all_gather | solution.py:77
  350.2 127.4 %reduce-scatter.6.cloned.1.call-start = ((), (), s32[]{:S(2)}) async-start(), calls=%async_computation.7 | async-start | bytes 2228224 | tf_op jit(solution)/shard_map/reduce_scatter | solution.py:78
  391.6 6.8 copy-start.2
  398.4 79.2 %copy-start.5 = (f32[8,256,16]{1,2,0:T(8,128)S(1)}, f32[8,256,16]{1,2,0:T(8,128)}, u32[]{:S(2)}) copy-start(f32[8,256,16]{1,2,0:T(8,128)} %broadcast_divide_fusion.1) | copy-start | bytes 393220
  398.4 149.9 %copy-start.6 = (f32[8,256,16]{1,2,0:T(8,128)S(1)}, f32[8,256,16]{1,2,0:T(8,128)}, u32[]{:S(2)}) copy-start(f32[8,256,16]{1,2,0:T(8,128)} %reduce-scatter.4.cloned.1.call-done) | copy-start | bytes 393220
  404.4 251.0 %all-gather.8.cloned.1.call-start = ((), (), s32[]{:S(2)}) async-start(), calls=%async_computation.8 | async-start | bytes 2228224 | tf_op jit(solution)/shard_map/all_gather | solution.py:77
  613.9 127.4 %reduce-scatter.8.cloned.1.call-start = ((), (), s32[]{:S(2)}) async-start(), calls=%async_computation.9 | async-start | bytes 2228224 | tf_op jit(solution)/shard_map/reduce_scatter | solution.py:78
  655.3 6.8 copy-start.3
Sparse Core Ops, SparseCore 0:
  31.1 46.3 all-gather.3
  140.4 73.5 reduce-scatter.3
  350.3 41.2 all-gather.5
  404.5 73.0 reduce-scatter.5
  614.0 41.2 all-gather.7
  668.2 73.0 reduce-scatter.7
where the time goes:
time: 822 us; the launch traced here: 821 us
  waiting for transfers between devices  390 us (47%)
  blocking collectives  323 us (39%)
  matrix products  38 us (5%)
  between operations  25.5 us (3%)
  other arithmetic  21.1 us (3%)
  local copies, waits for them, and re-layouts  17.1 us (2%)
    psum x5, blocking collectives, combine(): reduced = lax.psum(values, ('row', 'col'))  323 us
    reduce_scatter x3, waiting for transfers between devices, operate(): lax.psum_scatter(contract(full_vector), 'col', scatter_dimension=2, tiled...  220 us
    all_to_all x1, waiting for transfers between devices, local(): lax.all_to_all(outgoing, 'row', split_axis=0, concat_axis=0, tiled=True)  86.8 us
    all_gather x3, waiting for transfers between devices, operate(): full_vector = lax.all_gather(vector, 'col', axis=2, tiled=True)  82.6 us
    dot_general x3, matrix products, contract(): jnp.einsum('swia,sab->swib', left_pick, full_vector, precision=highest)  20.3 us
    dot_general x3, matrix products, contract(): return jnp.einsum('swib,swjb->sij', middle, right_pick, precision=highest)  17.6 us
  transfers between devices with their start and end apart: 7, of which 6 were waited for; matrix products, arithmetic and copies ran while one was open for 2% of the time, Pallas kernels for 0%

commit v1 on v0

--- a/solution.py
+++ b/solution.py
@@ -79,7 +79,7 @@
         return total_sum * start_mask
 
     def combine(values):
-        reduced = lax.psum(values, ("row", "col"))
+        reduced = lax.psum(lax.psum(values, "col"), "row")
         return reduced
 
     image_vec = operate(start_vec)

time: 822 us -> 754 us (0.917)
  blocking collectives: 323 us -> 259 us
    psum x5 -> x10, blocking collectives: 323 us -> 259 us  [combine(): reduced = lax.psum(lax.psum(values, 'col'), 'row')]
where the time goes in v1:
time: 754 us; the launch traced here: 753 us
  waiting for transfers between devices  386 us (51%)
  blocking collectives  259 us (34%)
  matrix products  38 us (5%)
  between operations  25.5 us (3%)
  other arithmetic  21.1 us (3%)
  local copies, waits for them, and re-layouts  17.1 us (2%)
    psum x10, blocking collectives, combine(): reduced = lax.psum(lax.psum(values, 'col'), 'row')  259 us
    reduce_scatter x3, waiting for transfers between devices, operate(): lax.psum_scatter(contract(full_vector), 'col', scatter_dimension=2, tiled...  220 us
    all_to_all x1, waiting for transfers between devices, local(): lax.all_to_all(outgoing, 'row', split_axis=0, concat_axis=0, tiled=True)  86.8 us
    all_gather x3, waiting for transfers between devices, operate(): full_vector = lax.all_gather(vector, 'col', axis=2, tiled=True)  78.7 us
    dot_general x3, matrix products, contract(): jnp.einsum('swia,sab->swib', left_pick, full_vector, precision=highest)  20.3 us
    dot_general x3, matrix products, contract(): return jnp.einsum('swib,swjb->sij', middle, right_pick, precision=highest)  17.6 us
  transfers between devices with their start and end apart: 7, of which 6 were waited for; matrix products, arithmetic and copies ran while one was open for 2% of the time, Pallas kernels for 0%

profile of v1, /device:TPU:1, one launch (start us, length us, event | category | flops | bytes accessed | tf_op | source)
XLA Modules:
  0.0 752.9 jit_solution(632695455833942023)
XLA Ops:
  7.2 0.9 eq.29
  8.1 0.2 compare_reduce_fusion
  8.4 0.1 copy.12
  8.5 0.1 reshape.147
  8.5 0.1 reshape.146
  8.7 0.1 copy.14
  8.8 0.1 reshape.149
  8.9 4.3 gather_fusion
  13.2 7.9 %select_multiply_fusion = f32[16,2,256,256]{3,2,1,0:T(8,128)} fusion(f32[16,2,256,256]{3,2,1,0:T(8,128)} %gather_fusion, f32[16]{0:T(128)S(1)} %reshape.149, pred[16]{0:T(512)(128)(4,1)S(1)} %compare_and_fusion.1), kind=kLoop, calls=%fused_computation.3 | loop fusion | flops 4194304 | bytes 16777296 | tf_op jit(solution)/shard_map/mul | solution.py:54
  21.1 6.4 all-to-all-start
  27.5 0.1 dynamic_slice.3
  27.6 0.1 fusion.51
  27.7 0.1 reshape.148
  27.8 0.2 reduce_window_sum.19
  27.9 0.1 reduce_window_sum.20
  28.0 0.2 select_reduce_fusion
  28.2 0.2 select_reduce_fusion.1
  28.4 0.1 compare_convert_fusion
  28.5 0.1 fusion.50
  28.6 0.7 multiply_multiply_fusion.3
  29.3 0.0 all-gather.4.cloned.1.call-update
  29.3 0.0 reduce-scatter.4.cloned.1.call-start
  29.4 0.1 copy.15
  29.5 4.9 gather_fusion.2
  34.4 0.1 compare_and_fusion.2
  34.5 86.8 %all-to-all-done = f32[16,2,256,256]{3,2,1,0:T(8,128)} async-done(((f32[16,2,256,256]{3,2,1,0:T(8,128)}), f32[16,2,256,256]{3,2,1,0:T(8,128)}, u32[]{:S(2)}, u32[]{:S(2)}) %all-to-all-start) | async-done | bytes 8388640 | tf_op jit(solution)/shard_map/all_to_all | solution.py:56
  121.4 6.2 gather_fusion.1
  127.6 6.8 fusion.13
  134.4 5.9 fusion.33
  140.2 0.0 reduce-scatter.4.cloned.1.call-update
  140.3 0.0 all-gather.6.cloned.1.call-start
  140.3 73.6 %reduce-scatter.4.cloned.1.call-done = f32[8,256,16]{1,2,0:T(8,128)} async-done(((f32[8,256,256]{1,2,0:T(8,128)}), f32[8,256,16]{1,2,0:T(8,128)}) %reduce-scatter.4.cloned.1.call-update) | async-done | bytes 131088 | tf_op jit(solution)/shard_map/reduce_scatter | solution.py:78
  213.9 1.6 multiply_reduce_fusion.4
  215.6 31.5 %all-reduce = (f32[]{:T(128)}, f32[]{:T(128)}) all-reduce(f32[]{:T(128)} %get-tuple-element.3, f32[]{:T(128)} %get-tuple-element.2), channel_id=1, replica_groups=mesh['row'=8,'col'=16] {'col'}, use_global_device_ids=true, to_apply=%region_14.15 | all-reduce | flops 2 | bytes 16 | tf_op jit(solution)/shard_map/psum | solution.py:82
  247.0 22.0 %all-reduce.1 = (f32[]{:T(128)}, f32[]{:T(128)}) all-reduce(f32[]{:T(128)} %get-tuple-element.6, f32[]{:T(128)} %get-tuple-element.7), channel_id=1, replica_groups=mesh['row'=8,'col'=16] {'row'}, use_global_device_ids=true, to_apply=%region_15.16 | all-reduce | flops 2 | bytes 16 | tf_op jit(solution)/shard_map/psum | solution.py:82
  271.0 1.6 multiply_reduce_fusion.2
  272.6 29.1 %psum.88 = f32[]{:T(128)} all-reduce(f32[]{:T(128)} %multiply_reduce_fusion.2), channel_id=1, replica_groups=mesh['row'=8,'col'=16] {'col'}, use_global_device_ids=true, to_apply=%region_17.18 | all-reduce | flops 1 | bytes 8 | tf_op jit(solution)/shard_map/psum | solution.py:82
  301.8 20.0 %psum.89 = f32[]{:T(128)} all-reduce(f32[]{:T(128)} %psum.88), channel_id=1, replica_groups=mesh['row'=8,'col'=16] {'row'}, use_global_device_ids=true, to_apply=%region_18.19 | all-reduce | flops 1 | bytes 8 | tf_op jit(solution)/shard_map/psum | solution.py:82
  322.4 1.7 broadcast_divide_fusion.1
  324.1 0.0 all-gather.6.cloned.1.call-update
  324.1 0.2 reduce-scatter.6.cloned.1.call-start
  324.4 39.4 %all-gather.6.cloned.1.call-done = f32[8,256,256]{1,2,0:T(8,128)} async-done(((f32[8,256,16]{1,2,0:T(8,128)}), f32[8,256,256]{1,2,0:T(8,128)}) %all-gather.6.cloned.1.call-update) | async-done | bytes 2097168 | tf_op jit(solution)/shard_map/all_gather | solution.py:77
  363.7 6.8 fusion.11
  370.6 5.9 fusion.38
  376.4 0.0 reduce-scatter.6.cloned.1.call-update
  376.5 0.0 all-gather.8.cloned.1.call-start
  376.5 73.2 %reduce-scatter.6.cloned.1.call-done = f32[8,256,16]{1,2,0:T(8,128)} async-done(((f32[8,256,256]{1,2,0:T(8,128)}), f32[8,256,16]{1,2,0:T(8,128)}) %reduce-scatter.6.cloned.1.call-update) | async-done | bytes 131088 | tf_op jit(solution)/shard_map/reduce_scatter | solution.py:78
  449.7 1.6 multiply_reduce_fusion.1
  451.3 31.5 %psum.90 = f32[]{:T(128)} all-reduce(f32[]{:T(128)} %multiply_reduce_fusion.1), channel_id=1, replica_groups=mesh['row'=8,'col'=16] {'col'}, use_global_device_ids=true, to_apply=%region_21.22 | all-reduce | flops 1 | bytes 8 | tf_op jit(solution)/shard_map/psum | solution.py:82
  482.8 21.9 %psum.91 = f32[]{:T(128)} all-reduce(f32[]{:T(128)} %psum.90), channel_id=1, replica_groups=mesh['row'=8,'col'=16] {'row'}, use_global_device_ids=true, to_apply=%region_22.23 | all-reduce | flops 1 | bytes 8 | tf_op jit(solution)/shard_map/psum | solution.py:82
  508.1 1.7 multiply_reduce_fusion
  509.7 29.1 %psum.92 = f32[]{:T(128)} all-reduce(f32[]{:T(128)} %get-tuple-element.10), channel_id=1, replica_groups=mesh['row'=8,'col'=16] {'col'}, use_global_device_ids=true, to_apply=%region_24.25 | all-reduce | flops 1 | bytes 8 | tf_op jit(solution)/shard_map/psum | solution.py:82
  538.8 20.1 %psum.93 = f32[]{:T(128)} all-reduce(f32[]{:T(128)} %psum.92), channel_id=1, replica_groups=mesh['row'=8,'col'=16] {'row'}, use_global_device_ids=true, to_apply=%region_25.26 | all-reduce | flops 1 | bytes 8 | tf_op jit(solution)/shard_map/psum | solution.py:82
  559.6 0.7 broadcast_divide_fusion
  560.2 0.0 all-gather.8.cloned.1.call-update
  560.3 0.3 reduce-scatter.8.cloned.1.call-start
  560.5 39.3 %all-gather.8.cloned.1.call-done = f32[8,256,256]{1,2,0:T(8,128)} async-done(((f32[8,256,16]{1,2,0:T(8,128)}), f32[8,256,256]{1,2,0:T(8,128)}) %all-gather.8.cloned.1.call-update) | async-done | bytes 2097168 | tf_op jit(solution)/shard_map/all_gather | solution.py:77
  599.9 6.8 fusion.9
  606.7 5.9 fusion.43
  612.6 73.3 %reduce-scatter.8.cloned.1.call-done = f32[8,256,16]{1,2,0:T(8,128)} async-done(((f32[8,256,256]{1,2,0:T(8,128)}), f32[8,256,16]{1,2,0:T(8,128)}) %reduce-scatter.8.cloned.1.call-update) | async-done | bytes 131088 | tf_op jit(solution)/shard_map/reduce_scatter | solution.py:78
  685.9 1.6 fusion.49
  687.5 31.5 %psum.94 = f32[]{:T(128)} all-reduce(f32[]{:T(128)} %fusion.49), channel_id=1, replica_groups=mesh['row'=8,'col'=16] {'col'}, use_global_device_ids=true, to_apply=%region_28.29 | all-reduce | flops 1 | bytes 8 | tf_op jit(solution)/shard_map/psum | solution.py:82
  719.0 21.9 %psum.95 = f32[]{:T(128)} all-reduce(f32[]{:T(128)} %psum.94), channel_id=1, replica_groups=mesh['row'=8,'col'=16] {'row'}, use_global_device_ids=true, to_apply=%region_29.30 | all-reduce | flops 1 | bytes 8 | tf_op jit(solution)/shard_map/psum | solution.py:82
  744.2 0.8 divide_multiply_fusion
  (45 shorter events, 0.2 us)
Async XLA Ops:
  7.2 1.7 copy-start
  21.1 6.4 copy-start.7
  21.1 6.9 copy-start.10
  21.1 7.0 copy-start.11
  21.1 7.1 copy-start.9
  21.1 7.5 copy-start.4
  21.1 8.3 %copy-start.8 = (s32[8,2]{0,1:T(2,128)S(1)}, s32[8,2]{0,1:T(2,128)}, u32[]{:S(2)}) copy-start(s32[8,2]{0,1:T(2,128)} %param.13) | copy-start | bytes 196
  21.1 100.3 %all-to-all-start = ((f32[16,2,256,256]{3,2,1,0:T(8,128)}), f32[16,2,256,256]{3,2,1,0:T(8,128)}, u32[]{:S(2)}, u32[]{:S(2)}) async-start(f32[16,2,256,256]{3,2,1,0:T(8,128)} %select_multiply_fusion), calls=%async_computation | async-start | bytes 16777216 | tf_op jit(solution)/shard_map/all_to_all | solution.py:56
  27.5 100.0 %all-gather.4.cloned.1.call-start = ((), (), s32[]{:S(2)}) async-start(), calls=%async_computation.4 | async-start | bytes 2228224 | tf_op jit(solution)/shard_map/all_gather | solution.py:77
  29.3 184.6 %reduce-scatter.4.cloned.1.call-start = ((), (), s32[]{:S(2)}) async-start(), calls=%async_computation.5 | async-start | bytes 2228224 | tf_op jit(solution)/shard_map/reduce_scatter | solution.py:78
  127.6 6.8 copy-start.1
  140.3 223.5 %all-gather.6.cloned.1.call-start = ((), (), s32[]{:S(2)}) async-start(), calls=%async_computation.6 | async-start | bytes 2228224 | tf_op jit(solution)/shard_map/all_gather | solution.py:77
  324.1 125.5 %reduce-scatter.6.cloned.1.call-start = ((), (), s32[]{:S(2)}) async-start(), calls=%async_computation.7 | async-start | bytes 2228224 | tf_op jit(solution)/shard_map/reduce_scatter | solution.py:78
  363.7 6.8 copy-start.2
  370.5 79.2 %copy-start.5 = (f32[8,256,16]{1,2,0:T(8,128)S(1)}, f32[8,256,16]{1,2,0:T(8,128)}, u32[]{:S(2)}) copy-start(f32[8,256,16]{1,2,0:T(8,128)} %broadcast_divide_fusion.1) | copy-start | bytes 393220
  370.5 137.5 %copy-start.6 = (f32[8,256,16]{1,2,0:T(8,128)S(1)}, f32[8,256,16]{1,2,0:T(8,128)}, u32[]{:S(2)}) copy-start(f32[8,256,16]{1,2,0:T(8,128)} %reduce-scatter.4.cloned.1.call-done) | copy-start | bytes 393220
  376.5 223.4 %all-gather.8.cloned.1.call-start = ((), (), s32[]{:S(2)}) async-start(), calls=%async_computation.8 | async-start | bytes 2228224 | tf_op jit(solution)/shard_map/all_gather | solution.py:77
  560.3 125.6 %reduce-scatter.8.cloned.1.call-start = ((), (), s32[]{:S(2)}) async-start(), calls=%async_computation.9 | async-start | bytes 2228224 | tf_op jit(solution)/shard_map/reduce_scatter | solution.py:78
  599.9 6.8 copy-start.3
Sparse Core Ops, SparseCore 0:
  31.1 46.3 all-gather.3
  140.4 73.5 reduce-scatter.3
  324.3 39.4 all-gather.5
  376.6 73.0 reduce-scatter.5
  560.4 39.4 all-gather.7
  612.7 73.1 reduce-scatter.7
